TPU v7x, 32 devices: a whole 2x2x4 slice. The times are simulated.
32 devices in a mesh: group: 2 (over x), col: 16 (over z, y, core).
Axes of the slice: x: 2, y: 2, z: 4, core: 2. Of those that a mesh axis runs over, the one named last changes fastest.
Arguments:
- homolog_embedding: bfloat16 [192, 64, 256], P('group', 'col'), parts along dimension 0, may hold values from -6 to 6
- left_factor_matrix: bfloat16 [256, 32], replicated, may hold values from -0.375 to 0.375
- right_factor_matrix: bfloat16 [256, 32], replicated, may hold values from -0.375 to 0.375
- decoder: bfloat16 [1024, 128], replicated, may hold values from -2 to 2
- pair_output_bias: float32 [128], replicated, may hold values from -3 to 3
- pair_output_gradient: bfloat16 [128, 64, 128], P('group', 'col'), parts along dimension 0, may hold values from -6 to 6
Outputs:
- first_operand_gradient: float32 [192, 64, 32], P('group', 'col'), parts along dimension 0
- second_operand_gradient: float32 [192, 64, 32], P('group', 'col'), parts along dimension 0
- alignment_gradient: bfloat16 [192, 64, 256], P('group', 'col'), parts along dimension 0
There are 2 independent parts, one for each index of `group`. A program takes and returns all parts, laid end to end along the dimension named above; an argument that names none is the same for every part. Nothing has to cross between parts.
All inputs are finite; a program needn't handle non-finite values.
Results may differ from a plain program's by a relative error of at most 0.0083.
Values may be sent and summed in bfloat16 or wider, within the bound.
A program may use at most 64 MiB of HBM per device.

v0:
```python
import jax
import jax.numpy as jnp
from jax import lax
from jax.sharding import PartitionSpec as P


def per_device(
    homolog_embedding,
    left_factor_matrix,
    right_factor_matrix,
    decoder,
    pair_output_bias,
    pair_output_gradient,
):
    alignment_row_count, local_residue_start, alignment_channel_width = homolog_embedding.shape
    operand_channel_width = left_factor_matrix.shape[1]
    channels = decoder.shape[1]
    residue_total_count = local_residue_start * lax.axis_size("col")
    reciprocal_rows = 1.0 / alignment_row_count
    block_res = local_residue_start * max(1, 96 // local_residue_start)
    alignment_flattened_rows = homolog_embedding.reshape(
        alignment_row_count * local_residue_start, alignment_channel_width
    )
    first_operand_rows = (
        jnp.dot(alignment_flattened_rows, left_factor_matrix, preferred_element_type=jnp.float32)
        .astype(jnp.bfloat16)
        .reshape(alignment_row_count, local_residue_start * operand_channel_width)
    )
    second_operand_rows = (
        jnp.dot(alignment_flattened_rows, right_factor_matrix, preferred_element_type=jnp.float32)
        .astype(jnp.bfloat16)
        .reshape(alignment_row_count, local_residue_start * operand_channel_width)
    )
    second_operand_local = second_operand_rows.reshape(
        alignment_row_count, local_residue_start, operand_channel_width
    )

    def outer_slopes(slope_rows, rows_by_length, col_span):
        backward = (
            jnp.dot(slope_rows, decoder.T, preferred_element_type=jnp.float32) * reciprocal_rows
        )
        return backward.astype(jnp.bfloat16).reshape(
            rows_by_length, col_span, operand_channel_width, operand_channel_width
        )

    offset_col = jnp.int32(0)
    second_operand_gradient = jnp.zeros(
        (alignment_row_count, local_residue_start, operand_channel_width), jnp.float32
    )
    stored = jnp.zeros((residue_total_count, local_residue_start * channels), jnp.bfloat16)
    left_segment = lax.all_gather(first_operand_rows, "col", axis=1, tiled=True)
    right_segment = lax.all_gather(second_operand_rows, "col", axis=1, tiled=True)
    right_whole = right_segment
    piece_res = left_segment.shape[1] // operand_channel_width
    first_res = offset_col // operand_channel_width
    collected = []
    for split_offset in range(0, piece_res, block_res):
        split_rows_by_length = min(block_res, piece_res - split_offset)
        split_left_block = left_segment[
            :,
            split_offset
            * operand_channel_width : (split_offset + split_rows_by_length)
            * operand_channel_width,
        ].reshape(alignment_row_count, split_rows_by_length, operand_channel_width)
        collected.append((split_rows_by_length, split_left_block, first_res + split_offset))
    for rows_by_length, left_block, first_row in collected:
        products = (
            jnp.einsum(
                "sic,sjd->ijcd",
                left_block,
                second_operand_local,
                preferred_element_type=jnp.float32,
            )
            * reciprocal_rows
        )
        products = products.astype(jnp.bfloat16).reshape(
            rows_by_length * local_residue_start, operand_channel_width * operand_channel_width
        )
        linear = jnp.dot(products, decoder, preferred_element_type=jnp.float32) + pair_output_bias
        upstream = lax.dynamic_slice_in_dim(pair_output_gradient, first_row, rows_by_length, 0)
        upstream = upstream.reshape(rows_by_length * local_residue_start, channels).astype(
            jnp.float32
        )
        accumulate_slope_rows = (upstream * 2.0 * jnp.maximum(linear, 0.0)).astype(jnp.bfloat16)
        stored = lax.dynamic_update_slice_in_dim(
            stored,
            accumulate_slope_rows.reshape(rows_by_length, local_residue_start * channels),
            first_row,
            0,
        )
        accumulate_slopes = outer_slopes(accumulate_slope_rows, rows_by_length, local_residue_start)
        second_operand_gradient = second_operand_gradient + jnp.einsum(
            "ijcd,sic->sjd", accumulate_slopes, left_block, preferred_element_type=jnp.float32
        )
    second_operand_gradient, stored, right_whole = (second_operand_gradient, stored, right_whole)
    received = lax.all_to_all(stored, "col", split_axis=0, concat_axis=1, tiled=True)
    right_all = right_whole.reshape(alignment_row_count, residue_total_count, operand_channel_width)
    col_span = local_residue_start * max(
        max(1, 96 // local_residue_start), lax.axis_size("col") // 8
    )
    first_operand_gradient = jnp.zeros(
        (alignment_row_count, local_residue_start, operand_channel_width), jnp.float32
    )
    for offset in range(0, residue_total_count, col_span):
        width_cols = min(col_span, residue_total_count - offset)
        slope_rows = received[:, offset * channels : (offset + width_cols) * channels].reshape(
            local_residue_start * width_cols, channels
        )
        slopes = outer_slopes(slope_rows, local_residue_start, width_cols)
        first_operand_gradient = first_operand_gradient + jnp.einsum(
            "ijcd,sjd->sic",
            slopes,
            right_all[:, offset : offset + width_cols],
            preferred_element_type=jnp.float32,
        )
    first_operand_gradient_step = first_operand_gradient.astype(jnp.bfloat16).reshape(
        alignment_row_count * local_residue_start, operand_channel_width
    )
    second_operand_gradient_step = second_operand_gradient.astype(jnp.bfloat16).reshape(
        alignment_row_count * local_residue_start, operand_channel_width
    )
    alignment_gradient = jnp.dot(
        first_operand_gradient_step, left_factor_matrix.T, preferred_element_type=jnp.float32
    ) + jnp.dot(
        second_operand_gradient_step, right_factor_matrix.T, preferred_element_type=jnp.float32
    )
    alignment_gradient = alignment_gradient.astype(jnp.bfloat16).reshape(
        alignment_row_count, local_residue_start, alignment_channel_width
    )
    return (first_operand_gradient, second_operand_gradient, alignment_gradient)


def solution(mesh):
    placed = (P("group", "col", None), P(), P(), P(), P(), P("group", "col", None))
    return jax.shard_map(
        per_device,
        mesh=mesh,
        in_specs=placed,
        out_specs=(P("group", "col", None), P("group", "col", None), P("group", "col", None)),
        check_vma=False,
    )
```

profile of v0, /device:TPU:0, one launch (start us, length us, event | category | flops | bytes accessed | tf_op | source)
XLA Modules:
  0.0 74.2 jit_solution(9161705522396213601)
XLA Ops:
  0.7 1.0 %reshape.53 = bf16[384,256]{1,0:T(8,128)(2,1)S(1)} reshape(bf16[96,4,256]{2,1,0:T(4,128)(2,1)} %param.6) | data formatting | bytes 393216 | tf_op jit(solution)/shard_map/reshape | solution.py:21
  1.7 0.9 %convolution_convert_fusion = bf16[384,32]{0,1:T(8,128)(2,1)S(1)} fusion(bf16[384,256]{1,0:T(8,128)(2,1)S(1)} %reshape.53, bf16[256,32]{0,1:T(8,128)(2,1)} %param.7), kind=kOutput, calls=%fused_computation.14 | convolution fusion | flops 6303744 | bytes 237568 | tf_op jit(solution)/shard_map/dot_general | solution.py:25
  2.8 24.2 %all_gather.7 = bf16[96,2048]{1,0:T(8,128)(2,1)S(1)} all-gather(bf16[96,128]{1,0:T(8,128)(2,1)S(1)} %reshape.56), channel_id=1, replica_groups=mesh['group'=2,'col'=16] {'col'}, dimensions={1}, use_global_device_ids=true | all-gather | bytes 417792 | tf_op jit(solution)/shard_map/all_gather | solution.py:51
  27.0 0.3 copy.32
  27.6 1.6 %fusion = bf16[64,4,32,32]{0,3,2,1:T(8,128)(2,1)} fusion(bf16[96,64,32]{0,2,1:T(8,128)(2,1)S(1)} %bitcast.48, bf16[96,4,32,1]{2,1,0,3:T(4,128)(2,1)S(1)} %bitcast.51), kind=kOutput, calls=%fused_computation.1 | convolution fusion | flops 50855936 | bytes 942080 | tf_op jit(solution)/shard_map/sic,sjd->ijcd/dot_general | solution.py:68
  29.3 4.2 %copy.35 = bf16[64,4,32,32]{3,2,1,0:T(8,128)(2,1)S(1)} copy(bf16[64,4,32,32]{0,3,2,1:T(8,128)(2,1)} %fusion) | data formatting | bytes 1048576 | tf_op jit(solution)/shard_map/convert_element_type | solution.py:76
  33.5 2.2 %reshape.58 = bf16[256,1024]{1,0:T(8,128)(2,1)S(1)} reshape(bf16[64,4,32,32]{3,2,1,0:T(8,128)(2,1)S(1)} %copy.35) | data formatting | bytes 1048576 | tf_op jit(solution)/shard_map/reshape | solution.py:76
  35.7 0.9 %convert_multiply_fusion = f32[64,4,128]{2,1,0:T(4,128)S(1)} fusion(bf16[64,4,128]{2,1,0:T(4,128)(2,1)} %param.11), kind=kLoop, calls=%fused_computation.18 | loop fusion | flops 65536 | bytes 196608 | tf_op jit(solution)/shard_map/mul | solution.py:84
  36.6 0.3 fusion.6
  36.9 0.7 all_to_all.12
  37.6 4.2 %all-to-all-start = ((bf16[16,4,512]{2,1,0:T(4,128)(2,1)}), bf16[16,4,512]{2,1,0:T(4,128)(2,1)}, u32[]{:S(2)}, u32[]{:S(2)}) async-start(bf16[16,4,512]{2,1,0:T(4,128)(2,1)} %all_to_all.12), calls=%async_computation | async-start | bytes 131072 | tf_op jit(solution)/shard_map/all_to_all | solution.py:96
  41.7 0.7 reshape.54
  42.5 0.3 fusion.2
  42.8 1.6 %reshape.61 = bf16[64,4,32,32]{3,2,1,0:T(8,128)(2,1)S(1)} reshape(bf16[256,1024]{1,0:T(8,128)(2,1)S(1)} %fusion.2) | data formatting | bytes 1048576 | tf_op jit(solution)/shard_map/reshape | solution.py:42
  44.4 1.3 %fusion.11 = (bf16[96,4,32]{0,2,1:T(8,128)(2,1)S(1)}, f32[96,4,32]{0,2,1:T(8,128)}) fusion(bf16[96,64,32,1]{0,2,3,1:T(8,128)(2,1)S(1)} %bitcast.49, bf16[64,4,32,32]{3,2,1,0:T(8,128)(2,1)S(1)} %reshape.61), kind=kOutput, calls=%fused_computation.21 | convolution fusion | flops 50343936 | bytes 991232 | tf_op jit(solution)/shard_map/ijcd,sic->sjd/dot_general | solution.py:92
  45.7 22.7 %all_gather.6 = bf16[96,2048]{1,0:T(8,128)(2,1)S(1)} all-gather(bf16[96,128]{1,0:T(8,128)(2,1)S(1)} %copy-done.1), channel_id=1, replica_groups=mesh['group'=2,'col'=16] {'col'}, dimensions={1}, use_global_device_ids=true | all-gather | bytes 417792 | tf_op jit(solution)/shard_map/all_gather | solution.py:52
  68.4 0.3 copy.29
  68.8 0.9 %copy.36 = bf16[4,16,512]{2,1,0:T(8,128)(2,1)S(1)} copy(bf16[4,16,512]{2,0,1:T(4,128)(2,1)} %bitcast.8) | data formatting | bytes 131072 | tf_op jit(solution)/shard_map/all_to_all | solution.py:96
  69.7 0.3 fusion.1
  70.0 1.6 %reshape.71 = bf16[4,64,32,32]{3,2,1,0:T(8,128)(2,1)S(1)} reshape(bf16[256,1024]{1,0:T(8,128)(2,1)S(1)} %fusion.1) | data formatting | bytes 1048576 | tf_op jit(solution)/shard_map/reshape | solution.py:42
  71.6 1.3 %fusion.10 = (bf16[96,4,32]{0,2,1:T(8,128)(2,1)S(1)}, f32[96,4,32]{0,2,1:T(8,128)}) fusion(bf16[96,64,32,1]{0,2,1,3:T(8,128)(2,1)S(1)} %bitcast.50, bf16[4,64,32,32]{3,2,1,0:T(8,128)(2,1)S(1)} %reshape.71), kind=kOutput, calls=%fused_computation.20 | convolution fusion | flops 50343936 | bytes 991232 | tf_op jit(solution)/shard_map/ijcd,sjd->sic/dot_general | solution.py:110
  73.1 0.2 fusion.12
  73.3 0.2 fusion.3
  73.5 0.7 reshape.64
  (18 shorter events, 0.9 us)
Async XLA Ops:
  0.6 36.0 %copy-start = (bf16[1024,128]{1,0:T(8,128)(2,1)S(1)}, bf16[1024,128]{1,0:T(8,128)(2,1)}, u32[]{:S(2)}) copy-start(bf16[1024,128]{1,0:T(8,128)(2,1)} %param.9) | copy-start | bytes 786436
  0.6 26.7 %copy-start.3 = (bf16[256,32]{0,1:T(8,128)(2,1)S(1)}, bf16[256,32]{0,1:T(8,128)(2,1)}, u32[]{:S(2)}) copy-start(bf16[256,32]{0,1:T(8,128)(2,1)} %param.8) | copy-start | bytes 49156
  33.5 3.1 %copy-start.4 = (f32[128]{0:T(128)S(1)}, f32[128]{0:T(128)}, u32[]{:S(2)}) copy-start(f32[128]{0:T(128)} %param.10) | copy-start | bytes 1540
  37.6 31.2 %all-to-all-start = ((bf16[16,4,512]{2,1,0:T(4,128)(2,1)}), bf16[16,4,512]{2,1,0:T(4,128)(2,1)}, u32[]{:S(2)}, u32[]{:S(2)}) async-start(bf16[16,4,512]{2,1,0:T(4,128)(2,1)} %all_to_all.12), calls=%async_computation | async-start | bytes 131072 | tf_op jit(solution)/shard_map/all_to_all | solution.py:96
  42.8 3.0 %copy-start.1 = (bf16[96,128]{1,0:T(8,128)(2,1)S(1)}, bf16[96,128]{1,0:T(8,128)(2,1)}, u32[]{:S(2)}) copy-start(bf16[96,128]{1,0:T(8,128)(2,1)} %reshape.54) | copy-start | bytes 73732
  70.0 3.1 %copy-start.2 = (bf16[256,32]{0,1:T(8,128)(2,1)S(1)}, bf16[256,32]{0,1:T(8,128)(2,1)}, u32[]{:S(2)}) copy-start(bf16[256,32]{0,1:T(8,128)(2,1)} %param.7) | copy-start | bytes 49156
where the time goes:
time: 74.6 us; the launch traced here: 74.2 us
  blocking collectives  46.9 us (63%)
  local copies, waits for them, and re-layouts  14.9 us (20%)
  matrix products  6.57 us (9%)
  starting transfers between devices  4.16 us (6%)
  other arithmetic  0.87 us (1%)
  between operations  0.86 us (1%)
    all_gather x1, blocking collectives, per_device(): left_segment = lax.all_gather(first_operand_rows, 'col', axis=1, tiled=True)  24.2 us
    all_gather x1, blocking collectives, per_device(): lax.all_gather(second_operand_rows, 'col', axis=1, tiled=True)  22.7 us
    convert_element_type x1, local copies, waits for them, and re-layouts, per_device(): products.astype(jnp.bfloat16)  4.19 us
    all_to_all x1, starting transfers between devices, per_device(): lax.all_to_all(stored, 'col', split_axis=0, concat_axis=1, tiled=True)  4.16 us
    reshape x2, local copies, waits for them, and re-layouts, outer_slopes(): backward.astype(jnp.bfloat16)  3.16 us
    reshape x1, local copies, waits for them, and re-layouts, per_device(): products.astype(jnp.bfloat16)  2.23 us
    dot_general x1, matrix products, per_device(): jnp.einsum('sic,sjd->ijcd', left_block, second_operand_local, preferred_e...  1.63 us
    all_to_all x2, local copies, waits for them, and re-layouts, per_device(): lax.all_to_all(stored, 'col', split_axis=0, concat_axis=1, tiled=True)  1.52 us
  transfers between devices with their start and end apart: 1, of which 0 were waited for; matrix products, arithmetic and copies ran while one was open for 6% of the time, Pallas kernels for 0%

commit v1 on v0

--- a/solution.py
+++ b/solution.py
@@ -2,6 +2,16 @@
 import jax.numpy as jnp
 from jax import lax
 from jax.sharding import PartitionSpec as P
+
+
+def around_the_ring(array, axis, along):
+    count = lax.axis_size(axis)
+    current, pieces = (array, [array])
+    for _ in range(count - 1):
+        current = lax.ppermute(current, axis, [(i, (i + 1) % count) for i in range(count)])
+        pieces.insert(0, current)
+    merged = jnp.concatenate(pieces, axis=along)
+    return jnp.roll(merged, (lax.axis_index(axis) + 1) * array.shape[along], axis=along)
 
 
 def per_device(
@@ -48,7 +58,7 @@
         (alignment_row_count, local_residue_start, operand_channel_width), jnp.float32
     )
     stored = jnp.zeros((residue_total_count, local_residue_start * channels), jnp.bfloat16)
-    left_segment = lax.all_gather(first_operand_rows, "col", axis=1, tiled=True)
+    left_segment = around_the_ring(first_operand_rows, "col", 1)
     right_segment = lax.all_gather(second_operand_rows, "col", axis=1, tiled=True)
     right_whole = right_segment
     piece_res = left_segment.shape[1] // operand_channel_width

time: 74.6 us -> 136 us (1.82)
  waiting for transfers between devices: 0.01 us -> 87.2 us
  blocking collectives: 46.9 us -> 19.1 us
    ppermute x0 -> x15, waiting for transfers between devices: none -> 81.8 us  [around_the_ring(): lax.ppermute(current, axis, [(i, (i + 1) % count) for i in range(count)])]
    all_gather x1 -> x0, blocking collectives: 24.2 us -> none  [per_device(): left_segment = lax.all_gather(first_operand_rows, 'col', axis=1, tiled=True)]
    all_to_all x1, waiting for transfers between devices: 0.01 us -> 5.43 us  [per_device(): lax.all_to_all(stored, 'col', split_axis=0, concat_axis=1, tiled=True)]
    all_gather x1, blocking collectives: 22.7 us -> 19.1 us  [per_device(): lax.all_gather(second_operand_rows, 'col', axis=1, tiled=True)]
  transfers between devices with their start and end apart: 1 -> 16, of which waited for: 0 -> 15; matrix products, arithmetic and copies ran while one was open for 6% -> 3% of each run, Pallas kernels for 0% -> 0%
where the time goes in v1:
time: 136 us
  waiting for transfers between devices  87.2 us (64%)
  blocking collectives  19.1 us (14%)
  local copies, waits for them, and re-layouts  15.4 us (11%)
  matrix products  7.32 us (5%)
  starting transfers between devices  4.74 us (3%)
    ppermute x15, waiting for transfers between devices, around_the_ring(): lax.ppermute(current, axis, [(i, (i + 1) % count) for i in range(count)])  81.8 us
    all_gather x1, blocking collectives, per_device(): lax.all_gather(second_operand_rows, 'col', axis=1, tiled=True)  19.1 us
    all_to_all x1, waiting for transfers between devices, per_device(): lax.all_to_all(stored, 'col', split_axis=0, concat_axis=1, tiled=True)  5.43 us
    convert_element_type x1, local copies, waits for them, and re-layouts, per_device(): products.astype(jnp.bfloat16)  4.19 us
    all_to_all x1, starting transfers between devices, per_device(): lax.all_to_all(stored, 'col', split_axis=0, concat_axis=1, tiled=True)  4.16 us
    reshape x2, local copies, waits for them, and re-layouts, outer_slopes(): backward.astype(jnp.bfloat16)  3.15 us
  transfers between devices with their start and end apart: 16, of which 15 were waited for; matrix products, arithmetic and copies ran while one was open for 3% of the time, Pallas kernels for 0%

profile of v1, /device:TPU:0, one launch (start us, length us, event | category | flops | bytes accessed | tf_op | source)
XLA Modules:
  0.0 135.6 jit_solution(7585390603305414176)
XLA Ops:
  3.4 6.5 %collective-permute-done = bf16[96,128]{1,0:T(8,128)(2,1)S(1)} collective-permute-done((bf16[96,128]{1,0:T(8,128)(2,1)S(1)}, bf16[96,128]{1,0:T(8,128)(2,1)S(1)}, u32[]{:S(2)}, u32[]{:S(2)}) %collective-permute-start) | collective-permute-done | bytes 24608 | tf_op jit(solution)/shard_map/ppermute | solution.py:11
  9.9 5.9 %collective-permute-done.1 = bf16[96,128]{1,0:T(8,128)(2,1)S(1)} collective-permute-done((bf16[96,128]{1,0:T(8,128)(2,1)S(1)}, bf16[96,128]{1,0:T(8,128)(2,1)S(1)}, u32[]{:S(2)}, u32[]{:S(2)}) %collective-permute-start.1) | collective-permute-done | bytes 24608 | tf_op jit(solution)/shard_map/ppermute | solution.py:11
  15.8 5.9 %collective-permute-done.2 = bf16[96,128]{1,0:T(8,128)(2,1)S(1)} collective-permute-done((bf16[96,128]{1,0:T(8,128)(2,1)S(1)}, bf16[96,128]{1,0:T(8,128)(2,1)S(1)}, u32[]{:S(2)}, u32[]{:S(2)}) %collective-permute-start.2) | collective-permute-done | bytes 24608 | tf_op jit(solution)/shard_map/ppermute | solution.py:11
  21.8 5.9 %collective-permute-done.3 = bf16[96,128]{1,0:T(8,128)(2,1)S(1)} collective-permute-done((bf16[96,128]{1,0:T(8,128)(2,1)S(1)}, bf16[96,128]{1,0:T(8,128)(2,1)S(1)}, u32[]{:S(2)}, u32[]{:S(2)}) %collective-permute-start.3) | collective-permute-done | bytes 24608 | tf_op jit(solution)/shard_map/ppermute | solution.py:11
  27.7 5.9 %collective-permute-done.4 = bf16[96,128]{1,0:T(8,128)(2,1)S(1)} collective-permute-done((bf16[96,128]{1,0:T(8,128)(2,1)S(1)}, bf16[96,128]{1,0:T(8,128)(2,1)S(1)}, u32[]{:S(2)}, u32[]{:S(2)}) %collective-permute-start.4) | collective-permute-done | bytes 24608 | tf_op jit(solution)/shard_map/ppermute | solution.py:11
  33.7 5.9 %collective-permute-done.5 = bf16[96,128]{1,0:T(8,128)(2,1)S(1)} collective-permute-done((bf16[96,128]{1,0:T(8,128)(2,1)S(1)}, bf16[96,128]{1,0:T(8,128)(2,1)S(1)}, u32[]{:S(2)}, u32[]{:S(2)}) %collective-permute-start.5) | collective-permute-done | bytes 24608 | tf_op jit(solution)/shard_map/ppermute | solution.py:11
  39.6 5.9 %collective-permute-done.6 = bf16[96,128]{1,0:T(8,128)(2,1)S(1)} collective-permute-done((bf16[96,128]{1,0:T(8,128)(2,1)S(1)}, bf16[96,128]{1,0:T(8,128)(2,1)S(1)}, u32[]{:S(2)}, u32[]{:S(2)}) %collective-permute-start.6) | collective-permute-done | bytes 24608 | tf_op jit(solution)/shard_map/ppermute | solution.py:11
  45.6 5.9 %collective-permute-done.7 = bf16[96,128]{1,0:T(8,128)(2,1)S(1)} collective-permute-done((bf16[96,128]{1,0:T(8,128)(2,1)S(1)}, bf16[96,128]{1,0:T(8,128)(2,1)S(1)}, u32[]{:S(2)}, u32[]{:S(2)}) %collective-permute-start.7) | collective-permute-done | bytes 24608 | tf_op jit(solution)/shard_map/ppermute | solution.py:11
  51.5 5.9 %collective-permute-done.8 = bf16[96,128]{1,0:T(8,128)(2,1)S(1)} collective-permute-done((bf16[96,128]{1,0:T(8,128)(2,1)S(1)}, bf16[96,128]{1,0:T(8,128)(2,1)S(1)}, u32[]{:S(2)}, u32[]{:S(2)}) %collective-permute-start.8) | collective-permute-done | bytes 24608 | tf_op jit(solution)/shard_map/ppermute | solution.py:11
  57.5 5.9 %collective-permute-done.9 = bf16[96,128]{1,0:T(8,128)(2,1)S(1)} collective-permute-done((bf16[96,128]{1,0:T(8,128)(2,1)S(1)}, bf16[96,128]{1,0:T(8,128)(2,1)S(1)}, u32[]{:S(2)}, u32[]{:S(2)}) %collective-permute-start.9) | collective-permute-done | bytes 24608 | tf_op jit(solution)/shard_map/ppermute | solution.py:11
  63.4 5.9 %collective-permute-done.10 = bf16[96,128]{1,0:T(8,128)(2,1)S(1)} collective-permute-done((bf16[96,128]{1,0:T(8,128)(2,1)S(1)}, bf16[96,128]{1,0:T(8,128)(2,1)S(1)}, u32[]{:S(2)}, u32[]{:S(2)}) %collective-permute-start.10) | collective-permute-done | bytes 24608 | tf_op jit(solution)/shard_map/ppermute | solution.py:11
  69.4 5.9 %collective-permute-done.11 = bf16[96,128]{1,0:T(8,128)(2,1)S(1)} collective-permute-done((bf16[96,128]{1,0:T(8,128)(2,1)S(1)}, bf16[96,128]{1,0:T(8,128)(2,1)S(1)}, u32[]{:S(2)}, u32[]{:S(2)}) %collective-permute-start.11) | collective-permute-done | bytes 24608 | tf_op jit(solution)/shard_map/ppermute | solution.py:11
  76.2 5.1 %collective-permute-done.12 = bf16[96,128]{1,0:T(8,128)(2,1)S(1)} collective-permute-done((bf16[96,128]{1,0:T(8,128)(2,1)S(1)}, bf16[96,128]{1,0:T(8,128)(2,1)S(1)}, u32[]{:S(2)}, u32[]{:S(2)}) %collective-permute-start.12) | collective-permute-done | bytes 24608 | tf_op jit(solution)/shard_map/ppermute | solution.py:11
  82.4 4.8 %collective-permute-done.13 = bf16[96,128]{1,0:T(8,128)(2,1)S(1)} collective-permute-done((bf16[96,128]{1,0:T(8,128)(2,1)S(1)}, bf16[96,128]{1,0:T(8,128)(2,1)S(1)}, u32[]{:S(2)}, u32[]{:S(2)}) %collective-permute-start.13) | collective-permute-done | bytes 24608 | tf_op jit(solution)/shard_map/ppermute | solution.py:11
  87.2 19.1 %all_gather.3 = bf16[96,2048]{1,0:T(8,128)(2,1)S(1)} all-gather(bf16[96,128]{1,0:T(8,128)(2,1)S(1)} %reshape.54), channel_id=1, replica_groups=mesh['group'=2,'col'=16] {'col'}, dimensions={1}, use_global_device_ids=true | all-gather | bytes 417792 | tf_op jit(solution)/shard_map/all_gather | solution.py:62
  108.1 1.7 %fusion = bf16[64,4,32,32]{0,3,2,1:T(8,128)(2,1)} fusion(bf16[96,64,32]{0,2,1:T(8,128)(2,1)S(1)} %bitcast.48, bf16[96,4,32,1]{2,1,0,3:T(4,128)(2,1)S(1)} %bitcast.51), kind=kOutput, calls=%fused_computation.1 | convolution fusion | flops 50855936 | bytes 942080 | tf_op jit(solution)/shard_map/sic,sjd->ijcd/dot_general | solution.py:78
  109.8 4.2 %copy.35 = bf16[64,4,32,32]{3,2,1,0:T(8,128)(2,1)S(1)} copy(bf16[64,4,32,32]{0,3,2,1:T(8,128)(2,1)} %fusion) | data formatting | bytes 1048576 | tf_op jit(solution)/shard_map/convert_element_type | solution.py:86
  114.0 2.2 %reshape.58 = bf16[256,1024]{1,0:T(8,128)(2,1)S(1)} reshape(bf16[64,4,32,32]{3,2,1,0:T(8,128)(2,1)S(1)} %copy.35) | data formatting | bytes 1048576 | tf_op jit(solution)/shard_map/reshape | solution.py:86
  117.5 1.6 %reshape.61 = bf16[64,4,32,32]{3,2,1,0:T(8,128)(2,1)S(1)} reshape(bf16[256,1024]{1,0:T(8,128)(2,1)S(1)} %fusion.2) | data formatting | bytes 1048576 | tf_op jit(solution)/shard_map/reshape | solution.py:52
  119.1 4.2 %all-to-all-start = ((bf16[16,4,512]{2,1,0:T(4,128)(2,1)}), bf16[16,4,512]{2,1,0:T(4,128)(2,1)}, u32[]{:S(2)}, u32[]{:S(2)}) async-start(bf16[16,4,512]{2,1,0:T(4,128)(2,1)} %all_to_all.12), calls=%async_computation | async-start | bytes 131072 | tf_op jit(solution)/shard_map/all_to_all | solution.py:106
  123.3 1.3 fusion.11
  124.7 5.4 %all-to-all-done = bf16[16,4,512]{2,1,0:T(4,128)(2,1)} async-done(((bf16[16,4,512]{2,1,0:T(4,128)(2,1)}), bf16[16,4,512]{2,1,0:T(4,128)(2,1)}, u32[]{:S(2)}, u32[]{:S(2)}) %all-to-all-start) | async-done | bytes 65568 | tf_op jit(solution)/shard_map/all_to_all | solution.py:106
  131.4 1.6 %reshape.71 = bf16[4,64,32,32]{3,2,1,0:T(8,128)(2,1)S(1)} reshape(bf16[256,1024]{1,0:T(8,128)(2,1)S(1)} %fusion.1) | data formatting | bytes 1048576 | tf_op jit(solution)/shard_map/reshape | solution.py:52
  133.0 1.3 fusion.10
  (80 shorter events, 10.3 us)
Async XLA Ops:
  0.6 115.6 %copy-start = (bf16[1024,128]{1,0:T(8,128)(2,1)S(1)}, bf16[1024,128]{1,0:T(8,128)(2,1)}, u32[]{:S(2)}) copy-start(bf16[1024,128]{1,0:T(8,128)(2,1)} %param.9) | copy-start | bytes 786436
  2.8 7.0 %collective-permute-start = (bf16[96,128]{1,0:T(8,128)(2,1)S(1)}, bf16[96,128]{1,0:T(8,128)(2,1)S(1)}, u32[]{:S(2)}, u32[]{:S(2)}) collective-permute-start(bf16[96,128]{1,0:T(8,128)(2,1)S(1)} %reshape.56), channel_id=1, source_target_pairs={{0,1},{1,2},{2,3},{3,4},{4,5},{5,6},{6,7},{7,8},{8,9},{9,10},{10,1... | collective-permute-start | bytes 73736 | tf_op jit(solution)/shard_map/ppermute | solution.py:11
  9.9 5.9 %collective-permute-start.1 = (bf16[96,128]{1,0:T(8,128)(2,1)S(1)}, bf16[96,128]{1,0:T(8,128)(2,1)S(1)}, u32[]{:S(2)}, u32[]{:S(2)}) collective-permute-start(bf16[96,128]{1,0:T(8,128)(2,1)S(1)} %collective-permute-done), channel_id=1, source_target_pairs={{0,1},{1,2},{2,3},{3,4},{4,5},{5,6},{6,7},{7,8},{8,9},{9,10},{10,1... | collective-permute-start | bytes 73736 | tf_op jit(solution)/shard_map/ppermute | solution.py:11
  15.8 5.9 %collective-permute-start.2 = (bf16[96,128]{1,0:T(8,128)(2,1)S(1)}, bf16[96,128]{1,0:T(8,128)(2,1)S(1)}, u32[]{:S(2)}, u32[]{:S(2)}) collective-permute-start(bf16[96,128]{1,0:T(8,128)(2,1)S(1)} %collective-permute-done.1), channel_id=1, source_target_pairs={{0,1},{1,2},{2,3},{3,4},{4,5},{5,6},{6,7},{7,8},{8,9},{9,10},{10,1... | collective-permute-start | bytes 73736 | tf_op jit(solution)/shard_map/ppermute | solution.py:11
  21.8 5.9 %collective-permute-start.3 = (bf16[96,128]{1,0:T(8,128)(2,1)S(1)}, bf16[96,128]{1,0:T(8,128)(2,1)S(1)}, u32[]{:S(2)}, u32[]{:S(2)}) collective-permute-start(bf16[96,128]{1,0:T(8,128)(2,1)S(1)} %collective-permute-done.2), channel_id=1, source_target_pairs={{0,1},{1,2},{2,3},{3,4},{4,5},{5,6},{6,7},{7,8},{8,9},{9,10},{10,1... | collective-permute-start | bytes 73736 | tf_op jit(solution)/shard_map/ppermute | solution.py:11
  27.7 5.9 %collective-permute-start.4 = (bf16[96,128]{1,0:T(8,128)(2,1)S(1)}, bf16[96,128]{1,0:T(8,128)(2,1)S(1)}, u32[]{:S(2)}, u32[]{:S(2)}) collective-permute-start(bf16[96,128]{1,0:T(8,128)(2,1)S(1)} %collective-permute-done.3), channel_id=1, source_target_pairs={{0,1},{1,2},{2,3},{3,4},{4,5},{5,6},{6,7},{7,8},{8,9},{9,10},{10,1... | collective-permute-start | bytes 73736 | tf_op jit(solution)/shard_map/ppermute | solution.py:11
  33.7 5.9 %collective-permute-start.5 = (bf16[96,128]{1,0:T(8,128)(2,1)S(1)}, bf16[96,128]{1,0:T(8,128)(2,1)S(1)}, u32[]{:S(2)}, u32[]{:S(2)}) collective-permute-start(bf16[96,128]{1,0:T(8,128)(2,1)S(1)} %collective-permute-done.4), channel_id=1, source_target_pairs={{0,1},{1,2},{2,3},{3,4},{4,5},{5,6},{6,7},{7,8},{8,9},{9,10},{10,1... | collective-permute-start | bytes 73736 | tf_op jit(solution)/shard_map/ppermute | solution.py:11
  39.6 5.9 %collective-permute-start.6 = (bf16[96,128]{1,0:T(8,128)(2,1)S(1)}, bf16[96,128]{1,0:T(8,128)(2,1)S(1)}, u32[]{:S(2)}, u32[]{:S(2)}) collective-permute-start(bf16[96,128]{1,0:T(8,128)(2,1)S(1)} %collective-permute-done.5), channel_id=1, source_target_pairs={{0,1},{1,2},{2,3},{3,4},{4,5},{5,6},{6,7},{7,8},{8,9},{9,10},{10,1... | collective-permute-start | bytes 73736 | tf_op jit(solution)/shard_map/ppermute | solution.py:11
  45.6 5.9 %collective-permute-start.7 = (bf16[96,128]{1,0:T(8,128)(2,1)S(1)}, bf16[96,128]{1,0:T(8,128)(2,1)S(1)}, u32[]{:S(2)}, u32[]{:S(2)}) collective-permute-start(bf16[96,128]{1,0:T(8,128)(2,1)S(1)} %collective-permute-done.6), channel_id=1, source_target_pairs={{0,1},{1,2},{2,3},{3,4},{4,5},{5,6},{6,7},{7,8},{8,9},{9,10},{10,1... | collective-permute-start | bytes 73736 | tf_op jit(solution)/shard_map/ppermute | solution.py:11
  51.5 5.9 %collective-permute-start.8 = (bf16[96,128]{1,0:T(8,128)(2,1)S(1)}, bf16[96,128]{1,0:T(8,128)(2,1)S(1)}, u32[]{:S(2)}, u32[]{:S(2)}) collective-permute-start(bf16[96,128]{1,0:T(8,128)(2,1)S(1)} %collective-permute-done.7), channel_id=1, source_target_pairs={{0,1},{1,2},{2,3},{3,4},{4,5},{5,6},{6,7},{7,8},{8,9},{9,10},{10,1... | collective-permute-start | bytes 73736 | tf_op jit(solution)/shard_map/ppermute | solution.py:11
  57.5 5.9 %collective-permute-start.9 = (bf16[96,128]{1,0:T(8,128)(2,1)S(1)}, bf16[96,128]{1,0:T(8,128)(2,1)S(1)}, u32[]{:S(2)}, u32[]{:S(2)}) collective-permute-start(bf16[96,128]{1,0:T(8,128)(2,1)S(1)} %collective-permute-done.8), channel_id=1, source_target_pairs={{0,1},{1,2},{2,3},{3,4},{4,5},{5,6},{6,7},{7,8},{8,9},{9,10},{10,1... | collective-permute-start | bytes 73736 | tf_op jit(solution)/shard_map/ppermute | solution.py:11
  63.4 5.9 %collective-permute-start.10 = (bf16[96,128]{1,0:T(8,128)(2,1)S(1)}, bf16[96,128]{1,0:T(8,128)(2,1)S(1)}, u32[]{:S(2)}, u32[]{:S(2)}) collective-permute-start(bf16[96,128]{1,0:T(8,128)(2,1)S(1)} %collective-permute-done.9), channel_id=1, source_target_pairs={{0,1},{1,2},{2,3},{3,4},{4,5},{5,6},{6,7},{7,8},{8,9},{9,10},{10,1... | collective-permute-start | bytes 73736 | tf_op jit(solution)/shard_map/ppermute | solution.py:11
  69.4 5.9 %collective-permute-start.11 = (bf16[96,128]{1,0:T(8,128)(2,1)S(1)}, bf16[96,128]{1,0:T(8,128)(2,1)S(1)}, u32[]{:S(2)}, u32[]{:S(2)}) collective-permute-start(bf16[96,128]{1,0:T(8,128)(2,1)S(1)} %collective-permute-done.10), channel_id=1, source_target_pairs={{0,1},{1,2},{2,3},{3,4},{4,5},{5,6},{6,7},{7,8},{8,9},{9,10},{10,1... | collective-permute-start | bytes 73736 | tf_op jit(solution)/shard_map/ppermute | solution.py:11
  75.3 5.9 %collective-permute-start.12 = (bf16[96,128]{1,0:T(8,128)(2,1)S(1)}, bf16[96,128]{1,0:T(8,128)(2,1)S(1)}, u32[]{:S(2)}, u32[]{:S(2)}) collective-permute-start(bf16[96,128]{1,0:T(8,128)(2,1)S(1)} %collective-permute-done.11), channel_id=1, source_target_pairs={{0,1},{1,2},{2,3},{3,4},{4,5},{5,6},{6,7},{7,8},{8,9},{9,10},{10,1... | collective-permute-start | bytes 73736 | tf_op jit(solution)/shard_map/ppermute | solution.py:11
  81.3 5.9 %collective-permute-start.13 = (bf16[96,128]{1,0:T(8,128)(2,1)S(1)}, bf16[96,128]{1,0:T(8,128)(2,1)S(1)}, u32[]{:S(2)}, u32[]{:S(2)}) collective-permute-start(bf16[96,128]{1,0:T(8,128)(2,1)S(1)} %collective-permute-done.12), channel_id=1, source_target_pairs={{0,1},{1,2},{2,3},{3,4},{4,5},{5,6},{6,7},{7,8},{8,9},{9,10},{10,1... | collective-permute-start | bytes 73736 | tf_op jit(solution)/shard_map/ppermute | solution.py:11
  87.2 20.1 %collective-permute-start.14 = (bf16[96,128]{1,0:T(8,128)(2,1)S(1)}, bf16[96,128]{1,0:T(8,128)(2,1)S(1)}, u32[]{:S(2)}, u32[]{:S(2)}) collective-permute-start(bf16[96,128]{1,0:T(8,128)(2,1)S(1)} %collective-permute-done.13), channel_id=1, source_target_pairs={{0,1},{1,2},{2,3},{3,4},{4,5},{5,6},{6,7},{7,8},{8,9},{9,10},{10,1... | collective-permute-start | bytes 73736 | tf_op jit(solution)/shard_map/ppermute | solution.py:11
  114.0 2.3 %copy-start.4 = (f32[128]{0:T(128)S(1)}, f32[128]{0:T(128)}, u32[]{:S(2)}) copy-start(f32[128]{0:T(128)} %param.10) | copy-start | bytes 1540
  119.1 11.1 %all-to-all-start = ((bf16[16,4,512]{2,1,0:T(4,128)(2,1)}), bf16[16,4,512]{2,1,0:T(4,128)(2,1)}, u32[]{:S(2)}, u32[]{:S(2)}) async-start(bf16[16,4,512]{2,1,0:T(4,128)(2,1)} %all_to_all.12), calls=%async_computation | async-start | bytes 131072 | tf_op jit(solution)/shard_map/all_to_all | solution.py:106
  124.6 8.4 %copy-start.1 = (bf16[96,2048]{0,1:T(8,128)(2,1)S(1)}, bf16[96,2048]{0,1:T(8,128)(2,1)}, u32[]{:S(2)}) copy-start(bf16[96,2048]{0,1:T(8,128)(2,1)} %copy.29) | copy-start | bytes 1179652
  131.4 3.1 %copy-start.2 = (bf16[256,32]{0,1:T(8,128)(2,1)S(1)}, bf16[256,32]{0,1:T(8,128)(2,1)}, u32[]{:S(2)}) copy-start(bf16[256,32]{0,1:T(8,128)(2,1)} %param.7) | copy-start | bytes 49156
  133.0 1.7 %copy-start.3 = (bf16[256,32]{0,1:T(8,128)(2,1)S(1)}, bf16[256,32]{0,1:T(8,128)(2,1)}, u32[]{:S(2)}) copy-start(bf16[256,32]{0,1:T(8,128)(2,1)} %param.8) | copy-start | bytes 49156
